TPU v7x, 32 devices: a whole 2x2x4 slice. The times are simulated.
32 devices in a mesh: groups: 2 (over y), seq: 4 (over z), section: 2 (over x), head: 2 (over core).
Axes of the slice: x: 2, y: 2, z: 4, core: 2. Of those that a mesh axis runs over, the one named last changes fastest.
Arguments:
- queries: bfloat16 [64, 64, 128], P(('groups', 'seq'), ('section', 'head')), parts along dimension 0, may hold values from -56 to 56
- key_cache: bfloat16 [15872, 8, 128], P(('groups', 'seq'), ('section', 'head')), parts along dimension 0, may hold values from -5 to 5
- value_cache: bfloat16 [15872, 8, 128], P(('groups', 'seq'), ('section', 'head')), parts along dimension 0, may hold values from -5 to 5
- new_features: bfloat16 [512, 8192], P(('groups', 'seq')), parts along dimension 0, may hold values from -60 to 60
- key_weight: bfloat16 [8192, 1024], P('seq', ('section', 'head')), may hold values from -2 to 2
- value_weight: bfloat16 [8192, 1024], P('seq', ('section', 'head')), may hold values from -0.0625 to 0.0625
- key_gain: float32 [128], replicated, may hold values from 0.5 to 2
- out_weight: bfloat16 [8192, 8192], P(('section', 'head'), 'seq'), may hold values from -0.5 to 0.5
- frame_length: int32 [128], P('groups'), parts along dimension 0, may hold values from 1 to 256, 8192 in all
- text_frame: int32 [64], P(('groups', 'seq')), parts along dimension 0, may hold values from 0 to 63
Outputs:
- layer_output: bfloat16 [64, 8192], P(('groups', 'section', 'head'), 'seq'), parts along dimension 0
- new_keys: bfloat16 [512, 8, 128], P(('groups', 'seq'), ('section', 'head')), parts along dimension 0
- new_values: bfloat16 [512, 8, 128], P(('groups', 'seq'), ('section', 'head')), parts along dimension 0
There are 2 independent parts, one for each index of `groups`. A program takes and returns all parts, laid end to end along the dimension named above; an argument that names none is the same for every part. Nothing has to cross between parts.
Inputs may be any that keep to these rules, and one draw needn't show every extreme that they name: `frame_length`: they sum to 8192.
All inputs are finite; a program needn't handle non-finite values.
Results may differ from a plain program's by a relative error of at most 0.015.
Values may be sent and summed in bfloat16 or wider, within the bound.
No kernel may reach another device: no remote copies, remote signals or barrier semaphores. Data moves between devices by JAX's collectives and lax.ppermute only.
A program may use at most 64 MiB of HBM per device.

v0:
```python
import jax
import jax.numpy as jnp
from jax import lax
from jax.sharding import PartitionSpec as P

masked_score = -1e30
norm_epsilon = 1e-05


def for_sending(shard):

    def short(part):
        return part.astype(jnp.bfloat16) if part.dtype == jnp.float32 else part

    return jax.tree.map(short, shard)


def passed_along(shard, axis, by):
    peers = lax.axis_size(axis)
    return lax.ppermute(shard, axis, [(i, (i + by) % peers) for i in range(peers)])


def visit_block(query_block, state, key_block, value_block, key_position, score_scale):
    row_peak, row_total, row_accum, row_limit = state
    block_rows, local_heads, head_depth = query_block.shape
    local_kv = key_block.shape[1]
    grouped = query_block.reshape(block_rows, local_kv, local_heads // local_kv, head_depth)
    scores = (
        jnp.einsum("rcgd,kcd->rcgk", grouped, key_block, preferred_element_type=jnp.float32)
        * score_scale
    )
    visible = (key_position[None, :] < row_limit[:, None])[:, None, None, :]
    block_peak = jnp.max(jnp.where(visible, scores, masked_score), axis=3)
    new_peak = jnp.maximum(row_peak, block_peak)
    weights = jnp.where(visible, jnp.exp(scores - new_peak[..., None]), 0.0)
    factor = jnp.exp(row_peak - new_peak)
    row_total = factor * row_total + jnp.sum(weights, axis=3)
    update = jnp.einsum(
        "rcgk,kcd->rcgd",
        weights.astype(jnp.bfloat16),
        value_block,
        preferred_element_type=jnp.float32,
    )
    row_accum = factor[..., None] * row_accum + update
    return (new_peak, row_total, row_accum, row_limit)


def fresh_state(query_block, row_limit, local_kv):
    block_rows, local_heads, head_depth = query_block.shape
    head_shape = (block_rows, local_kv, local_heads // local_kv)
    return (
        jnp.full(head_shape, masked_score, jnp.float32),
        jnp.zeros(head_shape, jnp.float32),
        jnp.zeros(head_shape + (head_depth,), jnp.float32),
        row_limit,
    )


def pass_forward(query_block, state, with_query):
    if with_query:
        query_block = jax.tree.map(
            lambda part, own: part.astype(own.dtype),
            passed_along(for_sending(query_block), "seq", 1),
            query_block,
        )
    state = passed_along(state, "seq", 1)
    return (query_block, state)


def cycle_attend(
    blocks, move_blocks, key_block, value_block, key_position, score_scale, cycle_length
):

    def one_visit(running, with_query):
        moved_list = []
        for member, move_block in zip(running, move_blocks):
            state_now = visit_block(
                member[0], member[1], key_block, value_block, key_position, score_scale
            )
            moved_list.append(move_block(member[0], state_now, with_query))
        return tuple(moved_list)

    def two_visits(turn_index, running):
        return one_visit(one_visit(running, True), True)

    running = lax.fori_loop(0, cycle_length // 2 - 1, two_visits, blocks)
    finished = one_visit(one_visit(running, True), False)
    outputs = []
    for member in finished:
        row_peak, row_total, row_accum, row_limit = member[1]
        attended = (row_accum / row_total[..., None]).astype(jnp.bfloat16)
        outputs.append(attended.reshape(attended.shape[0], -1))
    return outputs[0]


def on_device(
    queries,
    key_cache,
    value_cache,
    new_features,
    key_weight,
    value_weight,
    key_gain,
    out_weight,
    frame_length,
    text_frame,
):
    head_depth = key_cache.shape[2]
    local_kv = key_cache.shape[1]
    kv_width = key_weight.shape[1]
    new_rows = new_features.shape[0]
    spread = lax.all_to_all(new_features, "seq", split_axis=1, concat_axis=0, tiled=True)
    stacked_weight = jnp.concatenate((key_weight, value_weight), axis=1)
    summed = lax.psum_scatter(
        jnp.dot(spread, stacked_weight, preferred_element_type=jnp.float32).astype(jnp.bfloat16),
        "seq",
        scatter_dimension=0,
        tiled=True,
    ).astype(jnp.float32)
    key_raw = summed[:, :kv_width]
    value_raw = summed[:, kv_width:]
    key_heads = key_raw.reshape(new_rows, local_kv, head_depth)
    mean_square = jnp.mean(key_heads * key_heads, axis=2, keepdims=True)
    new_keys = (key_heads * lax.rsqrt(mean_square + norm_epsilon) * key_gain).astype(jnp.bfloat16)
    new_values = value_raw.reshape(new_rows, local_kv, head_depth).astype(jnp.bfloat16)
    key_block = jnp.concatenate((key_cache, new_keys), axis=0)
    value_block = jnp.concatenate((value_cache, new_values), axis=0)
    block_keys = key_block.shape[0]
    key_position = (
        lax.axis_index("seq") * block_keys + jnp.arange(block_keys, dtype=jnp.int32)
    ).astype(jnp.float32)
    frame_index = jnp.arange(frame_length.shape[0], dtype=jnp.int32)
    row_limit = jnp.sum(
        jnp.where(frame_index[None, :] <= text_frame[:, None], frame_length[None, :], 0), axis=1
    ).astype(jnp.float32)
    score_scale = head_depth ** (-0.5)
    cycle_length = lax.axis_size("seq")
    blocks = ((queries, fresh_state(queries, row_limit, local_kv)),)
    attended = cycle_attend(
        blocks, (pass_forward,), key_block, value_block, key_position, score_scale, cycle_length
    )
    partial_terms = jnp.dot(
        lax.all_gather(attended, "seq", axis=0, tiled=True),
        out_weight,
        preferred_element_type=jnp.float32,
    )
    layer_output = lax.psum_scatter(
        partial_terms.astype(jnp.bfloat16), ("section", "head"), scatter_dimension=0, tiled=True
    )
    return (layer_output, new_keys, new_values)


def solution(mesh):
    placed = (
        P(("groups", "seq"), ("section", "head"), None),
        P(("groups", "seq"), ("section", "head"), None),
        P(("groups", "seq"), ("section", "head"), None),
        P(("groups", "seq"), None),
        P("seq", ("section", "head")),
        P("seq", ("section", "head")),
        P(),
        P(("section", "head"), "seq"),
        P("groups"),
        P(("groups", "seq")),
    )
    return jax.shard_map(
        on_device,
        mesh=mesh,
        in_specs=placed,
        out_specs=(
            P(("groups", "section", "head"), "seq"),
            P(("groups", "seq"), ("section", "head"), None),
            P(("groups", "seq"), ("section", "head"), None),
        ),
        check_vma=False,
    )
```

profile of v0, /device:TPU:0, one launch (start us, length us, event | category | flops | bytes accessed | tf_op | source)
XLA Modules:
  0.0 143.7 jit_solution(10098577655566775212)
XLA Ops:
  7.2 2.3 %copy.138 = bf16[8,4,8,2048]{3,2,0,1:T(8,128)(2,1)} copy(bf16[8,4,8,2048]{3,2,1,0:T(8,128)(2,1)} %bitcast.94) | data formatting | bytes 2097152 | tf_op jit(solution)/shard_map/all_to_all | solution.py:112
  9.5 6.3 %all-to-all-start = ((bf16[64,4,2048]{2,0,1:T(8,128)(2,1)}), bf16[64,4,2048]{2,0,1:T(8,128)(2,1)S(1)}, u32[]{:S(2)}, u32[]{:S(2)}) async-start(bf16[64,4,2048]{2,0,1:T(8,128)(2,1)} %bitcast.90), calls=%async_computation | async-start | bytes 2097152 | tf_op jit(solution)/shard_map/all_to_all | solution.py:112
  15.9 0.2 select_reduce_fusion.4
  16.1 2.1 %collective-permute-start.1 = (f32[8]{0:T(128)S(1)}, f32[8]{0:T(128)S(1)}, u32[]{:S(2)}, u32[]{:S(2)}) collective-permute-start(f32[8]{0:T(128)S(1)} %convert_element_type.49), channel_id=1, source_target_pairs={{0,4},{4,8},{8,12},{12,0},{1,5},{5,9},{9,13},{13,1},{2,6},{6,10},{... | collective-permute-start | bytes 104 | tf_op jit(solution)/shard_map/while/body/eval_jaxpr/ppermute | solution.py:20
  18.1 1.5 %collective-permute-start.2 = (bf16[8,16,128]{2,1,0:T(8,128)(2,1)S(1)}, bf16[8,16,128]{2,1,0:T(8,128)(2,1)S(1)}, u32[]{:S(2)}, u32[]{:S(2)}) collective-permute-start(bf16[8,16,128]{2,1,0:T(8,128)(2,1)S(1)} %copy-done.3), channel_id=1, source_target_pairs={{0,4},{4,8},{8,12},{12,0},{1,5},{5,9},{9,13},{13,1},{2,6},{6,10},{... | collective-permute-start | bytes 98312 | tf_op jit(solution)/shard_map/while/body/eval_jaxpr/ppermute | solution.py:20
  19.6 22.7 %all-to-all-done = bf16[64,4,2048]{2,0,1:T(8,128)(2,1)S(1)} async-done(((bf16[64,4,2048]{2,0,1:T(8,128)(2,1)}), bf16[64,4,2048]{2,0,1:T(8,128)(2,1)S(1)}, u32[]{:S(2)}, u32[]{:S(2)}) %all-to-all-start) | async-done | bytes 1048608 | tf_op jit(solution)/shard_map/all_to_all | solution.py:112
  42.3 2.4 %fusion.11 = bf16[256,512]{0,1:T(8,128)(2,1)S(1)} fusion(bf16[256,2048]{1,0:T(8,128)(2,1)S(1)} %bitcast.95, bf16[2048,256]{1,0:T(8,128)(2,1)} %param.15, bf16[2048,256]{1,0:T(8,128)(2,1)} %param.14), kind=kOutput, calls=%fused_computation.14 | convolution fusion | flops 541196288 | bytes 3407872 | tf_op jit(solution)/shard_map/dot_general | solution.py:115
  44.7 0.0 copy-start.1
  44.7 0.8 copy.112
  45.5 0.0 reduce-scatter.7.cloned.1.call-update
  45.6 0.0 reduce-scatter.5.cloned.1.call-start
  45.6 0.1 copy.98
  45.8 0.2 copy-done.1
  46.0 0.1 copy.104
  46.1 0.1 collective-permute-start.4
  46.2 5.4 %collective-permute-done.4 = f32[8]{0:T(128)S(1)} collective-permute-done((f32[8]{0:T(128)S(1)}, f32[8]{0:T(128)S(1)}, u32[]{:S(2)}, u32[]{:S(2)}) %collective-permute-start.4) | collective-permute-done | bytes 64 | tf_op jit(solution)/shard_map/while/body/eval_jaxpr/ppermute | solution.py:20
  51.6 5.4 %collective-permute-done.7 = f32[8]{0:T(128)S(1)} collective-permute-done((f32[8]{0:T(128)S(1)}, f32[8]{0:T(128)S(1)}, u32[]{:S(2)}, u32[]{:S(2)}) %collective-permute-start.7) | collective-permute-done | bytes 64 | tf_op jit(solution)/shard_map/ppermute | solution.py:20
  56.9 0.1 broadcast_compare_fusion
  57.0 0.5 collective-permute-done.5
  57.5 7.0 %reduce-scatter.7.cloned.1.call-done = bf16[64,512]{1,0:T(8,128)(2,1)} async-done(((bf16[256,512]{1,0:T(8,128)(2,1)}), bf16[64,512]{1,0:T(8,128)(2,1)}) %reduce-scatter.7.cloned.1.call-update) | async-done | bytes 65552 | tf_op jit(solution)/shard_map/reduce_scatter | solution.py:114
  64.5 0.8 fusion.58
  65.3 0.1 multiply_reduce_fusion
  65.4 0.1 copy.96
  65.5 0.1 fusion.40
  65.6 0.6 select_reduce_fusion.3
  66.2 0.1 collective-permute-start
  66.3 0.4 fusion.15
  66.7 0.1 copy.114
  66.8 0.1 copy.105
  66.9 0.4 fusion.14
  67.3 1.3 collective-permute-start.9
  68.6 0.5 collective-permute-start.13
  69.1 0.6 select_reduce_fusion.2
  69.7 0.6 select_reduce_fusion.1
  70.3 0.6 select_reduce_fusion
  70.9 0.9 collective-permute-done
  71.7 2.4 %collective-permute-start.3 = (f32[8,2,8]{2,0,1:T(8,128)S(1)}, f32[8,2,8]{2,0,1:T(8,128)S(1)}, u32[]{:S(2)}, u32[]{:S(2)}) collective-permute-start(f32[8,2,8]{2,0,1:T(8,128)S(1)} %max.22), channel_id=1, source_target_pairs={{0,4},{4,8},{8,12},{12,0},{1,5},{5,9},{9,13},{13,1},{2,6},{6,10},{... | collective-permute-start | bytes 1544 | tf_op jit(solution)/shard_map/while/body/eval_jaxpr/ppermute | solution.py:20
  74.1 0.4 fusion.17
  74.5 0.1 collective-permute-start.14
  74.6 2.6 %collective-permute-done.3 = f32[8,2,8]{2,0,1:T(8,128)S(1)} collective-permute-done((f32[8,2,8]{2,0,1:T(8,128)S(1)}, f32[8,2,8]{2,0,1:T(8,128)S(1)}, u32[]{:S(2)}, u32[]{:S(2)}) %collective-permute-start.3) | collective-permute-done | bytes 544 | tf_op jit(solution)/shard_map/while/body/eval_jaxpr/ppermute | solution.py:20
  77.2 0.6 collective-permute-start.6
  77.7 0.4 fusion.19
  78.1 1.9 %collective-permute-done.14 = f32[8,2,8]{2,0,1:T(8,128)S(1)} collective-permute-done((f32[8,2,8]{2,0,1:T(8,128)S(1)}, f32[8,2,8]{2,0,1:T(8,128)S(1)}, u32[]{:S(2)}, u32[]{:S(2)}) %collective-permute-start.14) | collective-permute-done | bytes 544 | tf_op jit(solution)/shard_map/while/body/eval_jaxpr/ppermute | solution.py:20
  80.0 0.1 collective-permute-start.15
  80.0 2.7 %collective-permute-done.6 = f32[8,2,8]{2,0,1:T(8,128)S(1)} collective-permute-done((f32[8,2,8]{2,0,1:T(8,128)S(1)}, f32[8,2,8]{2,0,1:T(8,128)S(1)}, u32[]{:S(2)}, u32[]{:S(2)}) %collective-permute-start.6) | collective-permute-done | bytes 544 | tf_op jit(solution)/shard_map/ppermute | solution.py:20
  82.7 0.4 multiply_add_fusion.2
  83.1 0.1 collective-permute-start.10
  83.2 0.0 slice-start
  83.2 0.4 fusion.21
  83.6 5.7 %collective-permute-done.10 = f32[8,2,8,128]{3,2,0,1:T(8,128)S(1)} collective-permute-done((f32[8,2,8,128]{3,2,0,1:T(8,128)S(1)}, f32[8,2,8,128]{3,2,0,1:T(8,128)S(1)}, u32[]{:S(2)}, u32[]{:S(2)}) %collective-permute-start.10) | collective-permute-done | bytes 65568 | tf_op jit(solution)/shard_map/while/body/eval_jaxpr/ppermute | solution.py:20
  89.3 0.4 multiply_add_fusion.1
  89.7 0.1 collective-permute-start.11
  89.8 6.0 %collective-permute-done.11 = f32[8,2,8,128]{3,2,0,1:T(8,128)S(1)} collective-permute-done((f32[8,2,8,128]{3,2,0,1:T(8,128)S(1)}, f32[8,2,8,128]{3,2,0,1:T(8,128)S(1)}, u32[]{:S(2)}, u32[]{:S(2)}) %collective-permute-start.11) | collective-permute-done | bytes 65568 | tf_op jit(solution)/shard_map/ppermute | solution.py:20
  95.8 0.4 multiply_add_fusion
  96.2 0.1 collective-permute-start.12
  96.3 0.1 collective-permute-start.16
  96.3 6.1 %collective-permute-done.16 = f32[8,2,8]{2,0,1:T(8,128)S(1)} collective-permute-done((f32[8,2,8]{2,0,1:T(8,128)S(1)}, f32[8,2,8]{2,0,1:T(8,128)S(1)}, u32[]{:S(2)}, u32[]{:S(2)}) %collective-permute-start.16) | collective-permute-done | bytes 544 | tf_op jit(solution)/shard_map/ppermute | solution.py:20
  102.4 0.1 copy_bitcast_fusion.2
  102.6 13.3 %all_gather.3 = bf16[32,2048]{1,0:T(8,128)(2,1)S(1)} all-gather(bf16[8,2048]{1,0:T(8,128)(2,1)S(1)} %bitcast.98), channel_id=1, replica_groups=mesh['groups'=2,'seq'=4,'section'=2,'head'=2] {'seq'}, dimensions={0}, use_global_device_ids=true | all-gather | bytes 163840 | tf_op jit(solution)/shard_map/all_gather | solution.py:143
  115.9 2.2 %convolution_convert_fusion = bf16[32,2048]{1,0:T(8,128)(2,1)} fusion(bf16[32,2048]{1,0:T(8,128)(2,1)S(1)} %all_gather.3, bf16[2048,2048]{1,0:T(8,128)(2,1)S(1)} %bitcast.93), kind=kOutput, calls=%fused_computation.8 | convolution fusion | flops 268500992 | bytes 8650752 | tf_op jit(solution)/shard_map/dot_general | solution.py:142
  118.1 0.0 reduce-scatter.5.cloned.1.call-update
  118.1 0.6 copy.107
  118.8 0.7 copy.110
  119.5 17.3 %reduce-scatter.5.cloned.1.call-done = bf16[8,2048]{1,0:T(8,128)(2,1)} async-done(((bf16[32,2048]{1,0:T(8,128)(2,1)}), bf16[8,2048]{1,0:T(8,128)(2,1)}) %reduce-scatter.5.cloned.1.call-update) | async-done | bytes 32784 | tf_op jit(solution)/shard_map/reduce_scatter | solution.py:147
  (38 shorter events, 0.2 us)
Async XLA Ops:
  7.2 8.7 %copy-start.4 = (s32[64]{0:T(128)S(1)}, s32[64]{0:T(128)}, u32[]{:S(2)}) copy-start(s32[64]{0:T(128)} %param.18) | copy-start | bytes 772
  7.2 8.7 %copy-start.5 = (s32[8]{0:T(128)S(1)}, s32[8]{0:T(128)}, u32[]{:S(2)}) copy-start(s32[8]{0:T(128)} %param.19) | copy-start | bytes 100
  7.2 10.9 %copy-start.3 = (bf16[8,16,128]{2,1,0:T(8,128)(2,1)S(1)}, bf16[8,16,128]{2,1,0:T(8,128)(2,1)}, u32[]{:S(2)}) copy-start(bf16[8,16,128]{2,1,0:T(8,128)(2,1)} %param.10) | copy-start | bytes 98308
  9.5 32.8 %all-to-all-start = ((bf16[64,4,2048]{2,0,1:T(8,128)(2,1)}), bf16[64,4,2048]{2,0,1:T(8,128)(2,1)S(1)}, u32[]{:S(2)}, u32[]{:S(2)}) async-start(bf16[64,4,2048]{2,0,1:T(8,128)(2,1)} %bitcast.90), calls=%async_computation | async-start | bytes 2097152 | tf_op jit(solution)/shard_map/all_to_all | solution.py:112
  15.9 48.6 %reduce-scatter.7.cloned.1.call-start = ((), (), s32[]{:S(2)}) async-start(), calls=%async_computation.4 | async-start | bytes 327680 | tf_op jit(solution)/shard_map/reduce_scatter | solution.py:114
  16.1 30.1 %collective-permute-start.1 = (f32[8]{0:T(128)S(1)}, f32[8]{0:T(128)S(1)}, u32[]{:S(2)}, u32[]{:S(2)}) collective-permute-start(f32[8]{0:T(128)S(1)} %convert_element_type.49), channel_id=1, source_target_pairs={{0,4},{4,8},{8,12},{12,0},{1,5},{5,9},{9,13},{13,1},{2,6},{6,10},{... | collective-permute-start | bytes 104 | tf_op jit(solution)/shard_map/while/body/eval_jaxpr/ppermute | solution.py:20
  18.1 33.4 %collective-permute-start.2 = (bf16[8,16,128]{2,1,0:T(8,128)(2,1)S(1)}, bf16[8,16,128]{2,1,0:T(8,128)(2,1)S(1)}, u32[]{:S(2)}, u32[]{:S(2)}) collective-permute-start(bf16[8,16,128]{2,1,0:T(8,128)(2,1)S(1)} %copy-done.3), channel_id=1, source_target_pairs={{0,4},{4,8},{8,12},{12,0},{1,5},{5,9},{9,13},{13,1},{2,6},{6,10},{... | collective-permute-start | bytes 98312 | tf_op jit(solution)/shard_map/while/body/eval_jaxpr/ppermute | solution.py:20
  42.3 3.3 %copy-start = (bf16[1984,2,128]{2,1,0:T(2,128)(2,1)S(1)}, bf16[1984,2,128]{2,1,0:T(2,128)(2,1)}, u32[]{:S(2)}) copy-start(bf16[1984,2,128]{2,1,0:T(2,128)(2,1)} %param.11) | copy-start | bytes 3047428
  44.7 1.3 copy-start.1
  45.6 91.3 %reduce-scatter.5.cloned.1.call-start = ((), (), s32[]{:S(2)}) async-start(), calls=%async_computation.3 | async-start | bytes 163840 | tf_op jit(solution)/shard_map/reduce_scatter | solution.py:147
  45.6 19.9 %copy-start.2 = (f32[128]{0:T(128)S(1)}, f32[128]{0:T(128)}, u32[]{:S(2)}) copy-start(f32[128]{0:T(128)} %param.16) | copy-start | bytes 1540
  46.1 5.4 %collective-permute-start.4 = (f32[8]{0:T(128)S(1)}, f32[8]{0:T(128)S(1)}, u32[]{:S(2)}, u32[]{:S(2)}) collective-permute-start(f32[8]{0:T(128)S(1)} %collective-permute-done.1), channel_id=1, source_target_pairs={{0,4},{4,8},{8,12},{12,0},{1,5},{5,9},{9,13},{13,1},{2,6},{6,10},{... | collective-permute-start | bytes 104 | tf_op jit(solution)/shard_map/while/body/eval_jaxpr/ppermute | solution.py:20
  51.6 5.4 %collective-permute-start.7 = (f32[8]{0:T(128)S(1)}, f32[8]{0:T(128)S(1)}, u32[]{:S(2)}, u32[]{:S(2)}) collective-permute-start(f32[8]{0:T(128)S(1)} %collective-permute-done.4), channel_id=1, source_target_pairs={{0,4},{4,8},{8,12},{12,0},{1,5},{5,9},{9,13},{13,1},{2,6},{6,10},{... | collective-permute-start | bytes 104 | tf_op jit(solution)/shard_map/ppermute | solution.py:20
  51.6 5.9 %collective-permute-start.5 = (bf16[8,16,128]{2,1,0:T(8,128)(2,1)S(1)}, bf16[8,16,128]{2,1,0:T(8,128)(2,1)S(1)}, u32[]{:S(2)}, u32[]{:S(2)}) collective-permute-start(bf16[8,16,128]{2,1,0:T(8,128)(2,1)S(1)} %collective-permute-done.2), channel_id=1, source_target_pairs={{0,4},{4,8},{8,12},{12,0},{1,5},{5,9},{9,13},{13,1},{2,6},{6,10},{... | collective-permute-start | bytes 98312 | tf_op jit(solution)/shard_map/while/body/eval_jaxpr/ppermute | solution.py:20
  57.5 12.8 %collective-permute-start.8 = (bf16[8,16,128]{2,1,0:T(8,128)(2,1)S(1)}, bf16[8,16,128]{2,1,0:T(8,128)(2,1)S(1)}, u32[]{:S(2)}, u32[]{:S(2)}) collective-permute-start(bf16[8,16,128]{2,1,0:T(8,128)(2,1)S(1)} %collective-permute-done.5), channel_id=1, source_target_pairs={{0,4},{4,8},{8,12},{12,0},{1,5},{5,9},{9,13},{13,1},{2,6},{6,10},{... | collective-permute-start | bytes 98312 | tf_op jit(solution)/shard_map/ppermute | solution.py:20
  66.2 5.5 %collective-permute-start = (f32[8,2,8]{2,0,1:T(8,128)S(1)}, f32[8,2,8]{2,0,1:T(8,128)S(1)}, u32[]{:S(2)}, u32[]{:S(2)}) collective-permute-start(f32[8,2,8]{2,0,1:T(8,128)S(1)} %broadcast_maximum_fusion), channel_id=1, source_target_pairs={{0,4},{4,8},{8,12},{12,0},{1,5},{5,9},{9,13},{13,1},{2,6},{6,10},{... | collective-permute-start | bytes 1544 | tf_op jit(solution)/shard_map/while/body/eval_jaxpr/ppermute | solution.py:20
  67.3 15.4 %collective-permute-start.9 = (f32[8,2,8,128]{3,2,0,1:T(8,128)S(1)}, f32[8,2,8,128]{3,2,0,1:T(8,128)S(1)}, u32[]{:S(2)}, u32[]{:S(2)}) collective-permute-start(f32[8,2,8,128]{3,2,0,1:T(8,128)S(1)} %fusion.14), channel_id=1, source_target_pairs={{0,4},{4,8},{8,12},{12,0},{1,5},{5,9},{9,13},{13,1},{2,6},{6,10},{... | collective-permute-start | bytes 196616 | tf_op jit(solution)/shard_map/while/body/eval_jaxpr/ppermute | solution.py:20
  68.6 5.8 %collective-permute-start.13 = (f32[8,2,8]{2,0,1:T(8,128)S(1)}, f32[8,2,8]{2,0,1:T(8,128)S(1)}, u32[]{:S(2)}, u32[]{:S(2)}) collective-permute-start(f32[8,2,8]{2,0,1:T(8,128)S(1)} %get-tuple-element.67), channel_id=1, source_target_pairs={{0,4},{4,8},{8,12},{12,0},{1,5},{5,9},{9,13},{13,1},{2,6},{6,10},{... | collective-permute-start | bytes 1544 | tf_op jit(solution)/shard_map/while/body/eval_jaxpr/ppermute | solution.py:20
  71.7 5.4 %collective-permute-start.3 = (f32[8,2,8]{2,0,1:T(8,128)S(1)}, f32[8,2,8]{2,0,1:T(8,128)S(1)}, u32[]{:S(2)}, u32[]{:S(2)}) collective-permute-start(f32[8,2,8]{2,0,1:T(8,128)S(1)} %max.22), channel_id=1, source_target_pairs={{0,4},{4,8},{8,12},{12,0},{1,5},{5,9},{9,13},{13,1},{2,6},{6,10},{... | collective-permute-start | bytes 1544 | tf_op jit(solution)/shard_map/while/body/eval_jaxpr/ppermute | solution.py:20
  74.5 5.5 %collective-permute-start.14 = (f32[8,2,8]{2,0,1:T(8,128)S(1)}, f32[8,2,8]{2,0,1:T(8,128)S(1)}, u32[]{:S(2)}, u32[]{:S(2)}) collective-permute-start(f32[8,2,8]{2,0,1:T(8,128)S(1)} %get-tuple-element.58), channel_id=1, source_target_pairs={{0,4},{4,8},{8,12},{12,0},{1,5},{5,9},{9,13},{13,1},{2,6},{6,10},{... | collective-permute-start | bytes 1544 | tf_op jit(solution)/shard_map/while/body/eval_jaxpr/ppermute | solution.py:20
  77.2 5.5 %collective-permute-start.6 = (f32[8,2,8]{2,0,1:T(8,128)S(1)}, f32[8,2,8]{2,0,1:T(8,128)S(1)}, u32[]{:S(2)}, u32[]{:S(2)}) collective-permute-start(f32[8,2,8]{2,0,1:T(8,128)S(1)} %max.23), channel_id=1, source_target_pairs={{0,4},{4,8},{8,12},{12,0},{1,5},{5,9},{9,13},{13,1},{2,6},{6,10},{... | collective-permute-start | bytes 1544 | tf_op jit(solution)/shard_map/ppermute | solution.py:20
  80.0 9.8 %collective-permute-start.15 = (f32[8,2,8]{2,0,1:T(8,128)S(1)}, f32[8,2,8]{2,0,1:T(8,128)S(1)}, u32[]{:S(2)}, u32[]{:S(2)}) collective-permute-start(f32[8,2,8]{2,0,1:T(8,128)S(1)} %get-tuple-element.56), channel_id=1, source_target_pairs={{0,4},{4,8},{8,12},{12,0},{1,5},{5,9},{9,13},{13,1},{2,6},{6,10},{... | collective-permute-start | bytes 1544 | tf_op jit(solution)/shard_map/ppermute | solution.py:20
  83.1 6.1 %collective-permute-start.10 = (f32[8,2,8,128]{3,2,0,1:T(8,128)S(1)}, f32[8,2,8,128]{3,2,0,1:T(8,128)S(1)}, u32[]{:S(2)}, u32[]{:S(2)}) collective-permute-start(f32[8,2,8,128]{3,2,0,1:T(8,128)S(1)} %multiply_add_fusion.2), channel_id=1, source_target_pairs={{0,4},{4,8},{8,12},{12,0},{1,5},{5,9},{9,13},{13,1},{2,6},{6,10},{... | collective-permute-start | bytes 196616 | tf_op jit(solution)/shard_map/while/body/eval_jaxpr/ppermute | solution.py:20
  83.2 32.7 %slice-start = ((s8[8388608]{0:T(1024)(128)(4,1)}), s8[4194304]{0:T(1024)(128)(4,1)S(1)}, s32[]{:S(2)}) async-start(s8[8388608]{0:T(1024)(128)(4,1)} %bitcast.92), calls=%async_computation.5 | async-start | bytes 8388608
  89.2 26.7 %slice-start.1 = ((s8[8388608]{0:T(1024)(128)(4,1)}), s8[4194304]{0:T(1024)(128)(4,1)S(1)}, s32[]{:S(2)}) async-start(s8[8388608]{0:T(1024)(128)(4,1)} %bitcast.92), calls=%async_computation.6 | async-start | bytes 8388608
  89.7 6.1 %collective-permute-start.11 = (f32[8,2,8,128]{3,2,0,1:T(8,128)S(1)}, f32[8,2,8,128]{3,2,0,1:T(8,128)S(1)}, u32[]{:S(2)}, u32[]{:S(2)}) collective-permute-start(f32[8,2,8,128]{3,2,0,1:T(8,128)S(1)} %multiply_add_fusion.1), channel_id=1, source_target_pairs={{0,4},{4,8},{8,12},{12,0},{1,5},{5,9},{9,13},{13,1},{2,6},{6,10},{... | collective-permute-start | bytes 196616 | tf_op jit(solution)/shard_map/ppermute | solution.py:20
  96.2 6.2 %collective-permute-start.12 = (f32[8,2,8,128]{3,2,0,1:T(8,128)S(1)}, f32[8,2,8,128]{3,2,0,1:T(8,128)S(1)}, u32[]{:S(2)}, u32[]{:S(2)}) collective-permute-start(f32[8,2,8,128]{3,2,0,1:T(8,128)S(1)} %multiply_add_fusion), channel_id=1, source_target_pairs={{0,4},{4,8},{8,12},{12,0},{1,5},{5,9},{9,13},{13,1},{2,6},{6,10},{... | collective-permute-start | bytes 196616 | tf_op jit(solution)/shard_map/ppermute | solution.py:20
  96.3 6.2 %collective-permute-start.16 = (f32[8,2,8]{2,0,1:T(8,128)S(1)}, f32[8,2,8]{2,0,1:T(8,128)S(1)}, u32[]{:S(2)}, u32[]{:S(2)}) collective-permute-start(f32[8,2,8]{2,0,1:T(8,128)S(1)} %get-tuple-element.54), channel_id=1, source_target_pairs={{0,4},{4,8},{8,12},{12,0},{1,5},{5,9},{9,13},{13,1},{2,6},{6,10},{... | collective-permute-start | bytes 1544 | tf_op jit(solution)/shard_map/ppermute | solution.py:20
Sparse Core Ops, SparseCore 0:
  45.7 18.7 reduce-scatter.6
  118.3 18.5 reduce-scatter.4
where the time goes:
time: 144 us
  waiting for transfers between devices  84 us (58%)
  starting transfers between devices  15.2 us (11%)
  between operations  14.3 us (10%)
  blocking collectives  13.3 us (9%)
  matrix products  8.47 us (6%)
  local copies, waits for them, and re-layouts  5.37 us (4%)
  other arithmetic  2.99 us (2%)
    ppermute x17, waiting for transfers between devices, passed_along(): lax.ppermute(shard, axis, [(i, (i + by) % peers) for i in range(peers)])  36.9 us
    all_to_all x1, waiting for transfers between devices, on_device(): lax.all_to_all(new_features, 'seq', split_axis=1, concat_axis=0, tiled=True)  22.7 us
    reduce_scatter x1, waiting for transfers between devices, on_device(): lax.psum_scatter(partial_terms.astype(jnp.bfloat16), ('section', 'head'),...  17.3 us
    all_gather x1, blocking collectives, on_device(): lax.all_gather(attended, 'seq', axis=0, tiled=True)  13.3 us
    ppermute x17, starting transfers between devices, passed_along(): lax.ppermute(shard, axis, [(i, (i + by) % peers) for i in range(peers)])  8.83 us
    reduce_scatter x1, waiting for transfers between devices, on_device(): lax.psum_scatter(jnp.dot(spread, stacked_weight, preferred_element_type=j...  6.96 us
    all_to_all x1, starting transfers between devices, on_device(): lax.all_to_all(new_features, 'seq', split_axis=1, concat_axis=0, tiled=True)  6.35 us
  transfers between devices with their start and end apart: 20, of which 13 were waited for; matrix products, arithmetic and copies ran while one was open for 8% of the time, Pallas kernels for 0%

commit v1 on v0

--- a/solution.py
+++ b/solution.py
@@ -139,10 +139,15 @@
     attended = cycle_attend(
         blocks, (pass_forward,), key_block, value_block, key_position, score_scale, cycle_length
     )
+
+    def measure_the_bands(local_x):
+        return jnp.concatenate(
+            lax.all_to_all(jnp.stack([local_x for _ in range(lax.axis_size("seq"))]), "seq", 0, 0),
+            0,
+        )
+
     partial_terms = jnp.dot(
-        lax.all_gather(attended, "seq", axis=0, tiled=True),
-        out_weight,
-        preferred_element_type=jnp.float32,
+        measure_the_bands(attended), out_weight, preferred_element_type=jnp.float32
     )
     layer_output = lax.psum_scatter(
         partial_terms.astype(jnp.bfloat16), ("section", "head"), scatter_dimension=0, tiled=True

time: 144 us -> 139 us (0.965)
  blocking collectives: 13.3 us -> 8.31 us
    all_gather x1 -> x0, blocking collectives: 13.3 us -> none  [on_device(): lax.all_gather(attended, 'seq', axis=0, tiled=True)]
    all_to_all x0 -> x1, blocking collectives: none -> 8.31 us  [measure_the_bands(): lax.all_to_all(jnp.stack([local_x for _ in range(lax.axis_size('seq'))]),...]
where the time goes in v1:
time: 139 us
  waiting for transfers between devices  84 us (60%)
  starting transfers between devices  15.2 us (11%)
  between operations  14.3 us (10%)
  matrix products  8.47 us (6%)
  blocking collectives  8.31 us (6%)
  local copies, waits for them, and re-layouts  5.38 us (4%)
  other arithmetic  2.99 us (2%)
    ppermute x17, waiting for transfers between devices, passed_along(): lax.ppermute(shard, axis, [(i, (i + by) % peers) for i in range(peers)])  37.1 us
    all_to_all x1, waiting for transfers between devices, on_device(): lax.all_to_all(new_features, 'seq', split_axis=1, concat_axis=0, tiled=True)  22.7 us
    reduce_scatter x1, waiting for transfers between devices, on_device(): lax.psum_scatter(partial_terms.astype(jnp.bfloat16), ('section', 'head'),...  17.2 us
    ppermute x17, starting transfers between devices, passed_along(): lax.ppermute(shard, axis, [(i, (i + by) % peers) for i in range(peers)])  8.83 us
    all_to_all x1, blocking collectives, measure_the_bands(): lax.all_to_all(jnp.stack([local_x for _ in range(lax.axis_size('seq'))]),...  8.31 us
    reduce_scatter x1, waiting for transfers between devices, on_device(): lax.psum_scatter(jnp.dot(spread, stacked_weight, preferred_element_type=j...  6.96 us
    all_to_all x1, starting transfers between devices, on_device(): lax.all_to_all(new_features, 'seq', split_axis=1, concat_axis=0, tiled=True)  6.35 us
  transfers between devices with their start and end apart: 20, of which 13 were waited for; matrix products, arithmetic and copies ran while one was open for 8% of the time, Pallas kernels for 0%

profile of v1, /device:TPU:0, one launch (start us, length us, event | category | flops | bytes accessed | tf_op | source)
XLA Modules:
  0.0 138.7 jit_solution(10752726882065782231)
XLA Ops:
  7.2 2.3 %copy.138 = bf16[8,4,8,2048]{3,2,0,1:T(8,128)(2,1)} copy(bf16[8,4,8,2048]{3,2,1,0:T(8,128)(2,1)} %bitcast.96) | data formatting | bytes 2097152 | tf_op jit(solution)/shard_map/all_to_all | solution.py:112
  9.5 6.3 %all-to-all-start = ((bf16[64,4,2048]{2,0,1:T(8,128)(2,1)}), bf16[64,4,2048]{2,0,1:T(8,128)(2,1)S(1)}, u32[]{:S(2)}, u32[]{:S(2)}) async-start(bf16[64,4,2048]{2,0,1:T(8,128)(2,1)} %bitcast.92), calls=%async_computation | async-start | bytes 2097152 | tf_op jit(solution)/shard_map/all_to_all | solution.py:112
  15.9 0.2 select_reduce_fusion.4
  16.1 2.1 %collective-permute-start.1 = (f32[8]{0:T(128)S(1)}, f32[8]{0:T(128)S(1)}, u32[]{:S(2)}, u32[]{:S(2)}) collective-permute-start(f32[8]{0:T(128)S(1)} %convert_element_type.49), channel_id=1, source_target_pairs={{0,4},{4,8},{8,12},{12,0},{1,5},{5,9},{9,13},{13,1},{2,6},{6,10},{... | collective-permute-start | bytes 104 | tf_op jit(solution)/shard_map/while/body/eval_jaxpr/ppermute | solution.py:20
  18.1 1.5 %collective-permute-start.2 = (bf16[8,16,128]{2,1,0:T(8,128)(2,1)S(1)}, bf16[8,16,128]{2,1,0:T(8,128)(2,1)S(1)}, u32[]{:S(2)}, u32[]{:S(2)}) collective-permute-start(bf16[8,16,128]{2,1,0:T(8,128)(2,1)S(1)} %copy-done.3), channel_id=1, source_target_pairs={{0,4},{4,8},{8,12},{12,0},{1,5},{5,9},{9,13},{13,1},{2,6},{6,10},{... | collective-permute-start | bytes 98312 | tf_op jit(solution)/shard_map/while/body/eval_jaxpr/ppermute | solution.py:20
  19.6 22.7 %all-to-all-done = bf16[64,4,2048]{2,0,1:T(8,128)(2,1)S(1)} async-done(((bf16[64,4,2048]{2,0,1:T(8,128)(2,1)}), bf16[64,4,2048]{2,0,1:T(8,128)(2,1)S(1)}, u32[]{:S(2)}, u32[]{:S(2)}) %all-to-all-start) | async-done | bytes 1048608 | tf_op jit(solution)/shard_map/all_to_all | solution.py:112
  42.3 2.4 %fusion.11 = bf16[256,512]{0,1:T(8,128)(2,1)S(1)} fusion(bf16[256,2048]{1,0:T(8,128)(2,1)S(1)} %bitcast.97, bf16[2048,256]{1,0:T(8,128)(2,1)} %param.15, bf16[2048,256]{1,0:T(8,128)(2,1)} %param.14), kind=kOutput, calls=%fused_computation.14 | convolution fusion | flops 541196288 | bytes 3407872 | tf_op jit(solution)/shard_map/dot_general | solution.py:115
  44.7 0.0 copy-start.1
  44.7 0.8 copy.112
  45.5 0.0 reduce-scatter.7.cloned.1.call-update
  45.6 0.0 reduce-scatter.5.cloned.1.call-start
  45.6 0.1 copy.98
  45.8 0.2 copy-done.1
  46.0 0.1 copy.104
  46.1 0.1 collective-permute-start.4
  46.2 5.4 %collective-permute-done.4 = f32[8]{0:T(128)S(1)} collective-permute-done((f32[8]{0:T(128)S(1)}, f32[8]{0:T(128)S(1)}, u32[]{:S(2)}, u32[]{:S(2)}) %collective-permute-start.4) | collective-permute-done | bytes 64 | tf_op jit(solution)/shard_map/while/body/eval_jaxpr/ppermute | solution.py:20
  51.6 5.4 %collective-permute-done.7 = f32[8]{0:T(128)S(1)} collective-permute-done((f32[8]{0:T(128)S(1)}, f32[8]{0:T(128)S(1)}, u32[]{:S(2)}, u32[]{:S(2)}) %collective-permute-start.7) | collective-permute-done | bytes 64 | tf_op jit(solution)/shard_map/ppermute | solution.py:20
  56.9 0.1 broadcast_compare_fusion
  57.0 0.5 collective-permute-done.5
  57.5 7.0 %reduce-scatter.7.cloned.1.call-done = bf16[64,512]{1,0:T(8,128)(2,1)} async-done(((bf16[256,512]{1,0:T(8,128)(2,1)}), bf16[64,512]{1,0:T(8,128)(2,1)}) %reduce-scatter.7.cloned.1.call-update) | async-done | bytes 65552 | tf_op jit(solution)/shard_map/reduce_scatter | solution.py:114
  64.5 0.8 fusion.59
  65.3 0.1 multiply_reduce_fusion
  65.4 0.1 copy.96
  65.5 0.1 fusion.41
  65.6 0.6 select_reduce_fusion.3
  66.2 0.1 collective-permute-start
  66.3 0.4 fusion.15
  66.7 0.1 copy.114
  66.8 0.1 copy.105
  66.9 0.4 fusion.14
  67.3 1.3 collective-permute-start.9
  68.6 0.5 collective-permute-start.13
  69.1 0.6 select_reduce_fusion.2
  69.7 0.6 select_reduce_fusion.1
  70.3 0.6 select_reduce_fusion
  70.9 0.9 collective-permute-done
  71.7 2.4 %collective-permute-start.3 = (f32[8,2,8]{2,0,1:T(8,128)S(1)}, f32[8,2,8]{2,0,1:T(8,128)S(1)}, u32[]{:S(2)}, u32[]{:S(2)}) collective-permute-start(f32[8,2,8]{2,0,1:T(8,128)S(1)} %max.22), channel_id=1, source_target_pairs={{0,4},{4,8},{8,12},{12,0},{1,5},{5,9},{9,13},{13,1},{2,6},{6,10},{... | collective-permute-start | bytes 1544 | tf_op jit(solution)/shard_map/while/body/eval_jaxpr/ppermute | solution.py:20
  74.1 0.4 fusion.17
  74.5 0.1 collective-permute-start.14
  74.6 2.6 %collective-permute-done.3 = f32[8,2,8]{2,0,1:T(8,128)S(1)} collective-permute-done((f32[8,2,8]{2,0,1:T(8,128)S(1)}, f32[8,2,8]{2,0,1:T(8,128)S(1)}, u32[]{:S(2)}, u32[]{:S(2)}) %collective-permute-start.3) | collective-permute-done | bytes 544 | tf_op jit(solution)/shard_map/while/body/eval_jaxpr/ppermute | solution.py:20
  77.2 0.6 collective-permute-start.6
  77.7 0.4 fusion.19
  78.1 1.9 %collective-permute-done.14 = f32[8,2,8]{2,0,1:T(8,128)S(1)} collective-permute-done((f32[8,2,8]{2,0,1:T(8,128)S(1)}, f32[8,2,8]{2,0,1:T(8,128)S(1)}, u32[]{:S(2)}, u32[]{:S(2)}) %collective-permute-start.14) | collective-permute-done | bytes 544 | tf_op jit(solution)/shard_map/while/body/eval_jaxpr/ppermute | solution.py:20
  80.0 0.1 collective-permute-start.15
  80.0 2.7 %collective-permute-done.6 = f32[8,2,8]{2,0,1:T(8,128)S(1)} collective-permute-done((f32[8,2,8]{2,0,1:T(8,128)S(1)}, f32[8,2,8]{2,0,1:T(8,128)S(1)}, u32[]{:S(2)}, u32[]{:S(2)}) %collective-permute-start.6) | collective-permute-done | bytes 544 | tf_op jit(solution)/shard_map/ppermute | solution.py:20
  82.7 0.4 multiply_add_fusion.2
  83.1 0.1 collective-permute-start.10
  83.2 0.0 slice-start
  83.2 0.4 fusion.21
  83.6 5.7 %collective-permute-done.10 = f32[8,2,8,128]{3,2,0,1:T(8,128)S(1)} collective-permute-done((f32[8,2,8,128]{3,2,0,1:T(8,128)S(1)}, f32[8,2,8,128]{3,2,0,1:T(8,128)S(1)}, u32[]{:S(2)}, u32[]{:S(2)}) %collective-permute-start.10) | collective-permute-done | bytes 65568 | tf_op jit(solution)/shard_map/while/body/eval_jaxpr/ppermute | solution.py:20
  89.3 0.4 multiply_add_fusion.1
  89.7 0.1 collective-permute-start.11
  89.8 6.0 %collective-permute-done.11 = f32[8,2,8,128]{3,2,0,1:T(8,128)S(1)} collective-permute-done((f32[8,2,8,128]{3,2,0,1:T(8,128)S(1)}, f32[8,2,8,128]{3,2,0,1:T(8,128)S(1)}, u32[]{:S(2)}, u32[]{:S(2)}) %collective-permute-start.11) | collective-permute-done | bytes 65568 | tf_op jit(solution)/shard_map/ppermute | solution.py:20
  95.8 0.4 multiply_add_fusion
  96.2 0.1 collective-permute-start.12
  96.3 0.1 collective-permute-start.16
  96.3 6.3 %collective-permute-done.16 = f32[8,2,8]{2,0,1:T(8,128)S(1)} collective-permute-done((f32[8,2,8]{2,0,1:T(8,128)S(1)}, f32[8,2,8]{2,0,1:T(8,128)S(1)}, u32[]{:S(2)}, u32[]{:S(2)}) %collective-permute-start.16) | collective-permute-done | bytes 544 | tf_op jit(solution)/shard_map/ppermute | solution.py:20
  102.7 0.1 copy_bitcast_fusion.2
  102.8 8.3 %all_to_all.24 = bf16[4,8,2048]{2,1,0:T(8,128)(2,1)S(1)} all-to-all(bf16[4,8,2048]{2,1,0:T(8,128)(2,1)S(1)} %stack.3), channel_id=1, replica_groups=mesh['groups'=2,'seq'=4,'section'=2,'head'=2] {'seq'}, dimensions={0} | all-to-all | bytes 262144 | tf_op jit(solution)/shard_map/all_to_all | solution.py:145
  111.1 2.2 %convolution_convert_fusion = bf16[32,2048]{1,0:T(8,128)(2,1)} fusion(bf16[2048,2048]{1,0:T(8,128)(2,1)S(1)} %bitcast.95, bf16[4,8,2048]{2,1,0:T(8,128)(2,1)S(1)} %all_to_all.24), kind=kOutput, calls=%fused_computation.8 | convolution fusion | flops 268500992 | bytes 8650752 | tf_op jit(solution)/shard_map/dot_general | solution.py:149
  113.3 0.0 reduce-scatter.5.cloned.1.call-update
  113.3 0.6 copy.107
  114.0 0.7 copy.110
  114.7 17.2 %reduce-scatter.5.cloned.1.call-done = bf16[8,2048]{1,0:T(8,128)(2,1)} async-done(((bf16[32,2048]{1,0:T(8,128)(2,1)}), bf16[8,2048]{1,0:T(8,128)(2,1)}) %reduce-scatter.5.cloned.1.call-update) | async-done | bytes 32784 | tf_op jit(solution)/shard_map/reduce_scatter | solution.py:152
  (39 shorter events, 0.2 us)
Async XLA Ops:
  7.2 8.7 %copy-start.4 = (s32[64]{0:T(128)S(1)}, s32[64]{0:T(128)}, u32[]{:S(2)}) copy-start(s32[64]{0:T(128)} %param.18) | copy-start | bytes 772
  7.2 8.7 %copy-start.5 = (s32[8]{0:T(128)S(1)}, s32[8]{0:T(128)}, u32[]{:S(2)}) copy-start(s32[8]{0:T(128)} %param.19) | copy-start | bytes 100
  7.2 10.9 %copy-start.3 = (bf16[8,16,128]{2,1,0:T(8,128)(2,1)S(1)}, bf16[8,16,128]{2,1,0:T(8,128)(2,1)}, u32[]{:S(2)}) copy-start(bf16[8,16,128]{2,1,0:T(8,128)(2,1)} %param.10) | copy-start | bytes 98308
  9.5 32.8 %all-to-all-start = ((bf16[64,4,2048]{2,0,1:T(8,128)(2,1)}), bf16[64,4,2048]{2,0,1:T(8,128)(2,1)S(1)}, u32[]{:S(2)}, u32[]{:S(2)}) async-start(bf16[64,4,2048]{2,0,1:T(8,128)(2,1)} %bitcast.92), calls=%async_computation | async-start | bytes 2097152 | tf_op jit(solution)/shard_map/all_to_all | solution.py:112
  15.9 48.6 %reduce-scatter.7.cloned.1.call-start = ((), (), s32[]{:S(2)}) async-start(), calls=%async_computation.5 | async-start | bytes 327680 | tf_op jit(solution)/shard_map/reduce_scatter | solution.py:114
  16.1 30.1 %collective-permute-start.1 = (f32[8]{0:T(128)S(1)}, f32[8]{0:T(128)S(1)}, u32[]{:S(2)}, u32[]{:S(2)}) collective-permute-start(f32[8]{0:T(128)S(1)} %convert_element_type.49), channel_id=1, source_target_pairs={{0,4},{4,8},{8,12},{12,0},{1,5},{5,9},{9,13},{13,1},{2,6},{6,10},{... | collective-permute-start | bytes 104 | tf_op jit(solution)/shard_map/while/body/eval_jaxpr/ppermute | solution.py:20
  18.1 33.4 %collective-permute-start.2 = (bf16[8,16,128]{2,1,0:T(8,128)(2,1)S(1)}, bf16[8,16,128]{2,1,0:T(8,128)(2,1)S(1)}, u32[]{:S(2)}, u32[]{:S(2)}) collective-permute-start(bf16[8,16,128]{2,1,0:T(8,128)(2,1)S(1)} %copy-done.3), channel_id=1, source_target_pairs={{0,4},{4,8},{8,12},{12,0},{1,5},{5,9},{9,13},{13,1},{2,6},{6,10},{... | collective-permute-start | bytes 98312 | tf_op jit(solution)/shard_map/while/body/eval_jaxpr/ppermute | solution.py:20
  42.3 3.3 %copy-start = (bf16[1984,2,128]{2,1,0:T(2,128)(2,1)S(1)}, bf16[1984,2,128]{2,1,0:T(2,128)(2,1)}, u32[]{:S(2)}) copy-start(bf16[1984,2,128]{2,1,0:T(2,128)(2,1)} %param.11) | copy-start | bytes 3047428
  44.7 1.3 copy-start.1
  45.6 86.3 %reduce-scatter.5.cloned.1.call-start = ((), (), s32[]{:S(2)}) async-start(), calls=%async_computation.4 | async-start | bytes 163840 | tf_op jit(solution)/shard_map/reduce_scatter | solution.py:152
  45.6 19.9 %copy-start.2 = (f32[128]{0:T(128)S(1)}, f32[128]{0:T(128)}, u32[]{:S(2)}) copy-start(f32[128]{0:T(128)} %param.16) | copy-start | bytes 1540
  46.1 5.4 %collective-permute-start.4 = (f32[8]{0:T(128)S(1)}, f32[8]{0:T(128)S(1)}, u32[]{:S(2)}, u32[]{:S(2)}) collective-permute-start(f32[8]{0:T(128)S(1)} %collective-permute-done.1), channel_id=1, source_target_pairs={{0,4},{4,8},{8,12},{12,0},{1,5},{5,9},{9,13},{13,1},{2,6},{6,10},{... | collective-permute-start | bytes 104 | tf_op jit(solution)/shard_map/while/body/eval_jaxpr/ppermute | solution.py:20
  51.6 5.4 %collective-permute-start.7 = (f32[8]{0:T(128)S(1)}, f32[8]{0:T(128)S(1)}, u32[]{:S(2)}, u32[]{:S(2)}) collective-permute-start(f32[8]{0:T(128)S(1)} %collective-permute-done.4), channel_id=1, source_target_pairs={{0,4},{4,8},{8,12},{12,0},{1,5},{5,9},{9,13},{13,1},{2,6},{6,10},{... | collective-permute-start | bytes 104 | tf_op jit(solution)/shard_map/ppermute | solution.py:20
  51.6 5.9 %collective-permute-start.5 = (bf16[8,16,128]{2,1,0:T(8,128)(2,1)S(1)}, bf16[8,16,128]{2,1,0:T(8,128)(2,1)S(1)}, u32[]{:S(2)}, u32[]{:S(2)}) collective-permute-start(bf16[8,16,128]{2,1,0:T(8,128)(2,1)S(1)} %collective-permute-done.2), channel_id=1, source_target_pairs={{0,4},{4,8},{8,12},{12,0},{1,5},{5,9},{9,13},{13,1},{2,6},{6,10},{... | collective-permute-start | bytes 98312 | tf_op jit(solution)/shard_map/while/body/eval_jaxpr/ppermute | solution.py:20
  57.5 12.8 %collective-permute-start.8 = (bf16[8,16,128]{2,1,0:T(8,128)(2,1)S(1)}, bf16[8,16,128]{2,1,0:T(8,128)(2,1)S(1)}, u32[]{:S(2)}, u32[]{:S(2)}) collective-permute-start(bf16[8,16,128]{2,1,0:T(8,128)(2,1)S(1)} %collective-permute-done.5), channel_id=1, source_target_pairs={{0,4},{4,8},{8,12},{12,0},{1,5},{5,9},{9,13},{13,1},{2,6},{6,10},{... | collective-permute-start | bytes 98312 | tf_op jit(solution)/shard_map/ppermute | solution.py:20
  66.2 5.5 %collective-permute-start = (f32[8,2,8]{2,0,1:T(8,128)S(1)}, f32[8,2,8]{2,0,1:T(8,128)S(1)}, u32[]{:S(2)}, u32[]{:S(2)}) collective-permute-start(f32[8,2,8]{2,0,1:T(8,128)S(1)} %broadcast_maximum_fusion), channel_id=1, source_target_pairs={{0,4},{4,8},{8,12},{12,0},{1,5},{5,9},{9,13},{13,1},{2,6},{6,10},{... | collective-permute-start | bytes 1544 | tf_op jit(solution)/shard_map/while/body/eval_jaxpr/ppermute | solution.py:20
  67.3 15.4 %collective-permute-start.9 = (f32[8,2,8,128]{3,2,0,1:T(8,128)S(1)}, f32[8,2,8,128]{3,2,0,1:T(8,128)S(1)}, u32[]{:S(2)}, u32[]{:S(2)}) collective-permute-start(f32[8,2,8,128]{3,2,0,1:T(8,128)S(1)} %fusion.14), channel_id=1, source_target_pairs={{0,4},{4,8},{8,12},{12,0},{1,5},{5,9},{9,13},{13,1},{2,6},{6,10},{... | collective-permute-start | bytes 196616 | tf_op jit(solution)/shard_map/while/body/eval_jaxpr/ppermute | solution.py:20
  68.6 5.8 %collective-permute-start.13 = (f32[8,2,8]{2,0,1:T(8,128)S(1)}, f32[8,2,8]{2,0,1:T(8,128)S(1)}, u32[]{:S(2)}, u32[]{:S(2)}) collective-permute-start(f32[8,2,8]{2,0,1:T(8,128)S(1)} %get-tuple-element.67), channel_id=1, source_target_pairs={{0,4},{4,8},{8,12},{12,0},{1,5},{5,9},{9,13},{13,1},{2,6},{6,10},{... | collective-permute-start | bytes 1544 | tf_op jit(solution)/shard_map/while/body/eval_jaxpr/ppermute | solution.py:20
  71.7 5.4 %collective-permute-start.3 = (f32[8,2,8]{2,0,1:T(8,128)S(1)}, f32[8,2,8]{2,0,1:T(8,128)S(1)}, u32[]{:S(2)}, u32[]{:S(2)}) collective-permute-start(f32[8,2,8]{2,0,1:T(8,128)S(1)} %max.22), channel_id=1, source_target_pairs={{0,4},{4,8},{8,12},{12,0},{1,5},{5,9},{9,13},{13,1},{2,6},{6,10},{... | collective-permute-start | bytes 1544 | tf_op jit(solution)/shard_map/while/body/eval_jaxpr/ppermute | solution.py:20
  74.5 5.5 %collective-permute-start.14 = (f32[8,2,8]{2,0,1:T(8,128)S(1)}, f32[8,2,8]{2,0,1:T(8,128)S(1)}, u32[]{:S(2)}, u32[]{:S(2)}) collective-permute-start(f32[8,2,8]{2,0,1:T(8,128)S(1)} %get-tuple-element.58), channel_id=1, source_target_pairs={{0,4},{4,8},{8,12},{12,0},{1,5},{5,9},{9,13},{13,1},{2,6},{6,10},{... | collective-permute-start | bytes 1544 | tf_op jit(solution)/shard_map/while/body/eval_jaxpr/ppermute | solution.py:20
  77.2 5.5 %collective-permute-start.6 = (f32[8,2,8]{2,0,1:T(8,128)S(1)}, f32[8,2,8]{2,0,1:T(8,128)S(1)}, u32[]{:S(2)}, u32[]{:S(2)}) collective-permute-start(f32[8,2,8]{2,0,1:T(8,128)S(1)} %max.23), channel_id=1, source_target_pairs={{0,4},{4,8},{8,12},{12,0},{1,5},{5,9},{9,13},{13,1},{2,6},{6,10},{... | collective-permute-start | bytes 1544 | tf_op jit(solution)/shard_map/ppermute | solution.py:20
  80.0 9.8 %collective-permute-start.15 = (f32[8,2,8]{2,0,1:T(8,128)S(1)}, f32[8,2,8]{2,0,1:T(8,128)S(1)}, u32[]{:S(2)}, u32[]{:S(2)}) collective-permute-start(f32[8,2,8]{2,0,1:T(8,128)S(1)} %get-tuple-element.56), channel_id=1, source_target_pairs={{0,4},{4,8},{8,12},{12,0},{1,5},{5,9},{9,13},{13,1},{2,6},{6,10},{... | collective-permute-start | bytes 1544 | tf_op jit(solution)/shard_map/ppermute | solution.py:20
  83.1 6.1 %collective-permute-start.10 = (f32[8,2,8,128]{3,2,0,1:T(8,128)S(1)}, f32[8,2,8,128]{3,2,0,1:T(8,128)S(1)}, u32[]{:S(2)}, u32[]{:S(2)}) collective-permute-start(f32[8,2,8,128]{3,2,0,1:T(8,128)S(1)} %multiply_add_fusion.2), channel_id=1, source_target_pairs={{0,4},{4,8},{8,12},{12,0},{1,5},{5,9},{9,13},{13,1},{2,6},{6,10},{... | collective-permute-start | bytes 196616 | tf_op jit(solution)/shard_map/while/body/eval_jaxpr/ppermute | solution.py:20
  83.2 27.9 %slice-start = ((s8[8388608]{0:T(1024)(128)(4,1)}), s8[4194304]{0:T(1024)(128)(4,1)S(1)}, s32[]{:S(2)}) async-start(s8[8388608]{0:T(1024)(128)(4,1)} %bitcast.94), calls=%async_computation.6 | async-start | bytes 8388608
  89.2 21.8 %slice-start.1 = ((s8[8388608]{0:T(1024)(128)(4,1)}), s8[4194304]{0:T(1024)(128)(4,1)S(1)}, s32[]{:S(2)}) async-start(s8[8388608]{0:T(1024)(128)(4,1)} %bitcast.94), calls=%async_computation.7 | async-start | bytes 8388608
  89.7 6.1 %collective-permute-start.11 = (f32[8,2,8,128]{3,2,0,1:T(8,128)S(1)}, f32[8,2,8,128]{3,2,0,1:T(8,128)S(1)}, u32[]{:S(2)}, u32[]{:S(2)}) collective-permute-start(f32[8,2,8,128]{3,2,0,1:T(8,128)S(1)} %multiply_add_fusion.1), channel_id=1, source_target_pairs={{0,4},{4,8},{8,12},{12,0},{1,5},{5,9},{9,13},{13,1},{2,6},{6,10},{... | collective-permute-start | bytes 196616 | tf_op jit(solution)/shard_map/ppermute | solution.py:20
  96.2 6.4 %collective-permute-start.12 = (f32[8,2,8,128]{3,2,0,1:T(8,128)S(1)}, f32[8,2,8,128]{3,2,0,1:T(8,128)S(1)}, u32[]{:S(2)}, u32[]{:S(2)}) collective-permute-start(f32[8,2,8,128]{3,2,0,1:T(8,128)S(1)} %multiply_add_fusion), channel_id=1, source_target_pairs={{0,4},{4,8},{8,12},{12,0},{1,5},{5,9},{9,13},{13,1},{2,6},{6,10},{... | collective-permute-start | bytes 196616 | tf_op jit(solution)/shard_map/ppermute | solution.py:20
  96.3 6.4 %collective-permute-start.16 = (f32[8,2,8]{2,0,1:T(8,128)S(1)}, f32[8,2,8]{2,0,1:T(8,128)S(1)}, u32[]{:S(2)}, u32[]{:S(2)}) collective-permute-start(f32[8,2,8]{2,0,1:T(8,128)S(1)} %get-tuple-element.54), channel_id=1, source_target_pairs={{0,4},{4,8},{8,12},{12,0},{1,5},{5,9},{9,13},{13,1},{2,6},{6,10},{... | collective-permute-start | bytes 1544 | tf_op jit(solution)/shard_map/ppermute | solution.py:20
Sparse Core Ops, SparseCore 0:
  45.7 18.7 reduce-scatter.6
  113.4 18.3 reduce-scatter.4
